TPU v7x, 32 devices: a whole 2x2x4 slice. The times are simulated.
32 devices in a mesh: grp: 2 (over core), aux: 8 (over z, x), tr: 2 (over y).
Axes of the slice: x: 2, y: 2, z: 4, core: 2. Of those that a mesh axis runs over, the one named last changes fastest.
Arguments:
- trial_vectors: float32 [64, 8, 512], P('aux', None, 'tr'), may hold values from -6 to 6
- energy_val: float32 [64], P('aux'), may hold values from -1 to -0.2
- energy_cond: float32 [512], P('tr'), may hold values from 0.2 to 2
- coef_occ: bfloat16 [512, 64, 64], P('aux'), may hold values from -0.75 to 0.75
- coef_virt: bfloat16 [512, 512, 512], P('aux', 'tr'), may hold values from -0.01171875 to 0.01171875
- pair_coef: bfloat16 [64, 512, 512], P('aux', 'tr'), may hold values from -0.03125 to 0.03125
- live_aux: int32 [8], P('aux'), may hold values from 16 to 64, as said below
Outputs:
- applied: float32 [64, 8, 512], P('aux', None, 'tr')
- intersection: float32 [8, 8], replicated
Inputs may be any that keep to these rules, and one draw needn't show every extreme that they name: `live_aux`: equals 64 on at least one shard.
All inputs are finite; a program needn't handle non-finite values.
Results may differ from a plain program's by a relative error of at most 0.0048.
Values may be sent and summed in bfloat16 or wider, within the bound.
A program may use at most 64 MiB of HBM per device.

v0:
```python
import math
import jax
import jax.numpy as jnp
from jax import lax
from jax.sharding import PartitionSpec as P

V = 64
C = 512


def apply_hamiltonian(vectors, energy_gap, coef_occ, coef_virt, pair_coef, live_aux):
    rounded = vectors.astype(jnp.bfloat16)
    gathered = lax.all_gather(rounded, "aux", axis=0, tiled=True)
    group_index = lax.axis_index("grp")
    slots = coef_occ.shape[0]
    live_count = live_aux[0]
    zero_slot = jnp.zeros((), jnp.int32)
    range_high = jnp.where(group_index == 0, live_count, zero_slot)
    block_size = math.gcd(slots, 8)
    first_block = zero_slot // block_size
    last_block = (range_high + block_size - 1) // block_size
    full_vectors = gathered.shape[1]
    full_cond = coef_virt.shape[2]

    def one_block(block_index, running):
        slot_start = block_index * block_size
        piece_occ = lax.dynamic_slice_in_dim(coef_occ, slot_start, block_size, 0)
        piece_virt = lax.dynamic_slice_in_dim(coef_virt, slot_start, block_size, 0)
        slot_ids = slot_start + lax.iota(jnp.int32, block_size)
        keep_mask = ((slot_ids >= zero_slot) & (slot_ids < range_high)).astype(jnp.float32)
        blended = jnp.einsum(
            "puv,vkc->pukc", piece_occ, gathered, preferred_element_type=jnp.float32
        )
        blended = (blended * keep_mask[:, None, None, None]).astype(jnp.bfloat16)
        return running + jnp.einsum(
            "pukc,pcd->ukd", blended, piece_virt, preferred_element_type=jnp.float32
        )

    zero_term = jnp.zeros((gathered.shape[0], full_vectors, full_cond), jnp.float32)
    direct_term = lax.fori_loop(first_block, last_block, one_block, zero_term)
    direct_term = lax.psum_scatter(direct_term, "tr", scatter_dimension=2, tiled=True)
    direct_term = lax.psum_scatter(direct_term, "aux", scatter_dimension=0, tiled=True)
    is_exchange = group_index == 1
    projection = lax.cond(
        is_exchange,
        lambda: jnp.einsum("vcp,vkc->kp", pair_coef, rounded, preferred_element_type=jnp.float32),
        lambda: jnp.zeros((vectors.shape[1], pair_coef.shape[2]), jnp.float32),
    )
    projection = lax.psum(projection, ("aux", "tr"))
    projection_b = projection.astype(jnp.bfloat16)
    exchange_term = lax.cond(
        is_exchange,
        lambda: jnp.einsum(
            "vcp,kp->vkc", pair_coef, projection_b, preferred_element_type=jnp.float32
        ),
        lambda: jnp.zeros(vectors.shape, jnp.float32),
    )
    combined = lax.psum(direct_term + exchange_term, "grp")
    return energy_gap[:, None, :] * vectors + combined


def body(trial_vectors, energy_val, energy_cond, coef_occ, coef_virt, pair_coef, live_aux):
    energy_gap = energy_cond[None, :] - energy_val[:, None]
    applied_first = apply_hamiltonian(
        trial_vectors, energy_gap, coef_occ, coef_virt, pair_coef, live_aux
    )
    partial_intersection = jnp.einsum(
        "vkc,vjc->kj", trial_vectors, applied_first, precision=lax.Precision.HIGHEST
    )
    intersection = lax.psum(partial_intersection, ("aux", "tr")) / (V * C)
    residual = applied_first - jnp.einsum(
        "vkc,kj->vjc", trial_vectors, intersection, precision=lax.Precision.HIGHEST
    )
    correction = residual / energy_gap[:, None, :]
    applied = apply_hamiltonian(correction, energy_gap, coef_occ, coef_virt, pair_coef, live_aux)
    return (applied, intersection)


def solution(mesh):
    in_specs = (
        P("aux", None, "tr"),
        P("aux"),
        P("tr"),
        P("aux", None, None),
        P("aux", "tr", None),
        P("aux", "tr", None),
        P("aux"),
    )
    out_specs = (P("aux", None, "tr"), P())
    return jax.shard_map(body, mesh=mesh, in_specs=in_specs, out_specs=out_specs, check_vma=False)
```

profile of v0, /device:TPU:0, one launch (start us, length us, event | category | flops | bytes accessed | tf_op | source)
XLA Modules:
  0.0 438.0 jit_solution(5328799634057705139)
XLA Ops:
  8.7 32.5 %all_gather.6 = bf16[64,8,256]{2,1,0:T(8,128)(2,1)S(1)} all-gather(bf16[8,8,256]{2,1,0:T(8,128)(2,1)S(1)} %convert_element_type.40), channel_id=1, replica_groups=mesh['grp'=2,'aux'=8,'tr'=2] {'aux'}, dimensions={0}, use_global_device_ids=true | all-gather | bytes 294912 | tf_op jit(solution)/shard_map/all_gather | solution.py:13
  41.4 46.7 %while.20 = (s32[]{:T(128)}, f32[64,8,512]{2,1,0:T(8,128)S(1)}, s32[]{:T(128)}, bf16[64,64,64]{2,1,0:T(8,128)(2,1)}, bf16[64,8,256]{2,1,0:T(8,128)(2,1)S(1)}, /*...) while((s32[]{:T(128)}, f32[64,8,512]{2,1,0:T(8,128)S(1)}, ...), condition=%wide.region_1.2_spmd, body=%wide.region_0.1_spmd.sunk | while | flops 1210318848 | bytes 12976363 | solution.py:40
  41.4 1.7 fusion.77
  43.2 4.2 fusion.78
  47.4 1.6 fusion.77
  49.0 4.2 fusion.78
  53.2 1.6 fusion.77
  54.8 4.2 fusion.78
  59.0 1.6 fusion.77
  60.7 4.2 fusion.78
  64.9 1.6 fusion.77
  66.5 4.2 fusion.78
  70.7 1.6 fusion.77
  72.3 4.2 fusion.78
  76.5 1.6 fusion.77
  78.1 4.2 fusion.78
  82.3 1.6 fusion.77
  83.9 4.2 fusion.78
  89.2 18.8 %reduce-scatter.5.cloned.1.call-done = f32[64,8,256]{2,1,0:T(8,128)} async-done(((f32[64,8,512]{2,1,0:T(8,128)}), f32[64,8,256]{2,1,0:T(8,128)}) %reduce-scatter.5.cloned.1.call-update) | async-done | bytes 524304 | tf_op jit(solution)/shard_map/reduce_scatter | solution.py:41
  108.1 75.8 %psum.35 = bf16[8,512]{1,0:T(8,128)(2,1)S(1)} all-reduce(f32[8,512]{1,0:T(8,128)S(1)} %get-tuple-element.306), channel_id=1, replica_groups=mesh['grp'=2,'aux'=8,'tr'=2] {'aux','tr'}, use_global_device_ids=true, to_apply=%region_6.7 | all-reduce | flops 4096 | bytes 24576 | tf_op jit(solution)/shard_map/psum | solution.py:49
  184.0 1.5 add.77
  185.6 13.6 %all-reduce.3.cloned.1.call-done = f32[8,8,256]{2,1,0:T(8,128)} async-done(((f32[8,8,256]{2,1,0:T(8,128)}), f32[8,8,256]{2,1,0:T(8,128)}) %all-reduce.3.cloned.1.call-update) | async-done | bytes 65552 | tf_op jit(solution)/shard_map/psum | solution.py:58
  199.2 1.0 convolution_bitcast_fusion.5
  200.3 42.1 %psum.37 = f32[8,8]{0,1:T(8,128)S(1)} all-reduce(f32[8,8]{0,1:T(8,128)S(1)} %convolution_bitcast_fusion.5), channel_id=1, replica_groups=mesh['grp'=2,'aux'=8,'tr'=2] {'aux','tr'}, use_global_device_ids=true, to_apply=%region_10.11 | all-reduce | flops 64 | bytes 512 | tf_op jit(solution)/shard_map/psum | solution.py:70
  242.4 1.0 fusion.52
  243.5 30.8 %all_gather.7 = bf16[64,8,256]{2,1,0:T(8,128)(2,1)S(1)} all-gather(bf16[8,8,256]{2,1,0:T(8,128)(2,1)S(1)} %get-tuple-element.150), channel_id=1, replica_groups=mesh['grp'=2,'aux'=8,'tr'=2] {'aux'}, dimensions={0}, use_global_device_ids=true | all-gather | bytes 294912 | tf_op jit(solution)/shard_map/all_gather | solution.py:13
  274.3 46.6 %while.21 = (s32[]{:T(128)}, f32[64,8,512]{2,1,0:T(8,128)S(1)}, s32[]{:T(128)}, bf16[64,64,64]{2,1,0:T(8,128)(2,1)}, bf16[64,8,256]{2,1,0:T(8,128)(2,1)S(1)}, /*...) while((s32[]{:T(128)}, f32[64,8,512]{2,1,0:T(8,128)S(1)}, ...), condition=%wide.region_12.13_spmd, body=%wide.region_11.12_spmd.sunk | while | flops 1210318848 | bytes 12976363 | solution.py:40
  274.4 1.6 fusion.83
  276.0 4.2 fusion.84
  280.2 1.6 fusion.83
  281.8 4.2 fusion.84
  286.0 1.6 fusion.83
  287.6 4.2 fusion.84
  291.8 1.6 fusion.83
  293.4 4.2 fusion.84
  297.6 1.6 fusion.83
  299.3 4.2 fusion.84
  303.5 1.6 fusion.83
  305.1 4.2 fusion.84
  309.3 1.6 fusion.83
  310.9 4.2 fusion.84
  315.1 1.6 fusion.83
  316.7 4.2 fusion.84
  322.0 16.4 %reduce-scatter.9.cloned.1.call-done = f32[64,8,256]{2,1,0:T(8,128)} async-done(((f32[64,8,512]{2,1,0:T(8,128)}), f32[64,8,256]{2,1,0:T(8,128)}) %reduce-scatter.9.cloned.1.call-update) | async-done | bytes 524304 | tf_op jit(solution)/shard_map/reduce_scatter | solution.py:41
  338.4 76.0 %psum.38 = bf16[8,512]{1,0:T(8,128)(2,1)S(1)} all-reduce(f32[8,512]{1,0:T(8,128)S(1)} %get-tuple-element.308), channel_id=1, replica_groups=mesh['grp'=2,'aux'=8,'tr'=2] {'aux','tr'}, use_global_device_ids=true, to_apply=%region_17.18 | all-reduce | flops 4096 | bytes 24576 | tf_op jit(solution)/shard_map/psum | solution.py:49
  414.4 1.5 add.79
  416.6 13.1 %all-reduce.5.cloned.1.call-done = f32[8,8,256]{2,1,0:T(8,128)} async-done(((f32[8,8,256]{2,1,0:T(8,128)}), f32[8,8,256]{2,1,0:T(8,128)}) %all-reduce.5.cloned.1.call-update) | async-done | bytes 65552 | tf_op jit(solution)/shard_map/psum | solution.py:58
  429.6 1.5 multiply_add_fusion
  (56 shorter events, 4.3 us)
Async XLA Ops:
  7.2 100.8 %reduce-scatter.5.cloned.1.call-start = ((), (), s32[]{:S(2)}) async-start(), calls=%async_computation.4 | async-start | bytes 1572864 | tf_op jit(solution)/shard_map/reduce_scatter | solution.py:41
  41.4 66.7 %copy-start = (bf16[8,256,512]{2,1,0:T(8,128)(2,1)S(1)}, bf16[8,256,512]{2,1,0:T(8,128)(2,1)}, u32[]{:S(2)}) copy-start(bf16[8,256,512]{2,1,0:T(8,128)(2,1)} %param.24) | copy-start | bytes 6291460
  88.1 1.0 copy-start.2
  89.1 94.8 %reduce-scatter.7.cloned.1.call-start = ((), (), s32[]{:S(2)}) async-start(), calls=%async_computation.5 | async-start | bytes 589824 | tf_op jit(solution)/shard_map/reduce_scatter | solution.py:42
  108.0 91.2 %all-reduce.3.cloned.1.call-start = ((), (), s32[]{:S(2)}) async-start(), calls=%async_computation.6 | async-start | bytes 131072 | tf_op jit(solution)/shard_map/psum | solution.py:58
  108.1 77.5 %copy-start.4 = (f32[256]{0:T(256)S(1)}, f32[256]{0:T(256)}, u32[]{:S(2)}) copy-start(f32[256]{0:T(256)} %param.21) | copy-start | bytes 3076
  108.1 77.5 %copy-start.5 = (f32[8]{0:T(128)S(1)}, f32[8]{0:T(128)}, u32[]{:S(2)}) copy-start(f32[8]{0:T(128)} %param.20) | copy-start | bytes 100
  108.1 91.1 %copy-start.3 = (f32[8,8,256]{2,1,0:T(8,128)S(1)}, f32[8,8,256]{2,1,0:T(8,128)}, u32[]{:S(2)}) copy-start(f32[8,8,256]{2,1,0:T(8,128)} %param.19) | copy-start | bytes 196612
  185.5 152.9 %reduce-scatter.9.cloned.1.call-start = ((), (), s32[]{:S(2)}) async-start(), calls=%async_computation.7 | async-start | bytes 1572864 | tf_op jit(solution)/shard_map/reduce_scatter | solution.py:41
  320.9 1.0 copy-start.1
  321.9 92.5 %reduce-scatter.11.cloned.1.call-start = ((), (), s32[]{:S(2)}) async-start(), calls=%async_computation.8 | async-start | bytes 589824 | tf_op jit(solution)/shard_map/reduce_scatter | solution.py:42
  338.4 91.3 %all-reduce.5.cloned.1.call-start = ((), (), s32[]{:S(2)}) async-start(), calls=%async_computation.9 | async-start | bytes 131072 | tf_op jit(solution)/shard_map/psum | solution.py:58
Sparse Core Ops, SparseCore 0:
  89.3 18.6 reduce-scatter.4
  111.3 62.6 reduce-scatter.6
  185.6 13.5 all-reduce.2
  322.0 16.2 reduce-scatter.8
  341.5 62.6 reduce-scatter.10
  416.0 13.5 all-reduce.4
where the time goes:
time: 439 us; the launch traced here: 438 us
  blocking collectives  257 us (59%)
  matrix products  94.6 us (22%)
  waiting for transfers between devices  61.9 us (14%)
  between operations  14.9 us (3%)
  other arithmetic  5.46 us (1%)
    psum x2, blocking collectives, apply_hamiltonian(): projection = lax.psum(projection, ('aux', 'tr'))  152 us
    dot_general x16, matrix products, one_block(): jnp.einsum('pukc,pcd->ukd', blended, piece_virt, preferred_element_type=j...  67 us
    all_gather x2, blocking collectives, apply_hamiltonian(): gathered = lax.all_gather(rounded, 'aux', axis=0, tiled=True)  63.3 us
    psum x1, blocking collectives, body(): intersection = lax.psum(partial_intersection, ('aux', 'tr')) / (V * C)  42.1 us
    reduce_scatter x2, waiting for transfers between devices, apply_hamiltonian(): lax.psum_scatter(direct_term, 'tr', scatter_dimension=2, tiled=True)  35.1 us
    psum x2, waiting for transfers between devices, apply_hamiltonian(): combined = lax.psum(direct_term + exchange_term, 'grp')  26.7 us
    dot_general x16, matrix products, one_block(): jnp.einsum('puv,vkc->pukc', piece_occ, gathered, preferred_element_type=j...  25.6 us
  transfers between devices with their start and end apart: 6, of which 4 were waited for; matrix products, arithmetic and copies ran while one was open for 0% of the time, Pallas kernels for 0%

commit v1 on v0

--- a/solution.py
+++ b/solution.py
@@ -67,7 +67,7 @@
     partial_intersection = jnp.einsum(
         "vkc,vjc->kj", trial_vectors, applied_first, precision=lax.Precision.HIGHEST
     )
-    intersection = lax.psum(partial_intersection, ("aux", "tr")) / (V * C)
+    intersection = jnp.sum(lax.all_gather(partial_intersection, ("aux", "tr")), axis=0) / (V * C)
     residual = applied_first - jnp.einsum(
         "vkc,kj->vjc", trial_vectors, intersection, precision=lax.Precision.HIGHEST
     )

time: 439 us -> 420 us (0.957)
  matrix products: 94.6 us -> 75.8 us
    psum x1 -> x0, blocking collectives: 42.1 us -> none  [body(): intersection = lax.psum(partial_intersection, ('aux', 'tr')) / (V * C)]
    all_gather x0 -> x1, blocking collectives: none -> 41.4 us  [body(): lax.all_gather(partial_intersection, ('aux', 'tr'))]
    dot_general x16, matrix products: 67 us -> 48.1 us  [one_block(): jnp.einsum('pukc,pcd->ukd', blended, piece_virt, preferred_element_type=j...]
where the time goes in v1:
time: 420 us; the launch traced here: 419 us
  blocking collectives  256 us (61%)
  matrix products  75.8 us (18%)
  waiting for transfers between devices  61.9 us (15%)
  between operations  15 us (4%)
  other arithmetic  5.47 us (1%)
    psum x2, blocking collectives, apply_hamiltonian(): projection = lax.psum(projection, ('aux', 'tr'))  152 us
    all_gather x2, blocking collectives, apply_hamiltonian(): gathered = lax.all_gather(rounded, 'aux', axis=0, tiled=True)  63.3 us
    dot_general x16, matrix products, one_block(): jnp.einsum('pukc,pcd->ukd', blended, piece_virt, preferred_element_type=j...  48.1 us
    all_gather x1, blocking collectives, body(): lax.all_gather(partial_intersection, ('aux', 'tr'))  41.4 us
    reduce_scatter x2, waiting for transfers between devices, apply_hamiltonian(): lax.psum_scatter(direct_term, 'tr', scatter_dimension=2, tiled=True)  35.1 us
    psum x2, waiting for transfers between devices, apply_hamiltonian(): combined = lax.psum(direct_term + exchange_term, 'grp')  26.7 us
    dot_general x16, matrix products, one_block(): jnp.einsum('puv,vkc->pukc', piece_occ, gathered, preferred_element_type=j...  25.6 us
  transfers between devices with their start and end apart: 6, of which 4 were waited for; matrix products, arithmetic and copies ran while one was open for 0% of the time, Pallas kernels for 0%

profile of v1, /device:TPU:0, one launch (start us, length us, event | category | flops | bytes accessed | tf_op | source)
XLA Modules:
  0.0 418.6 jit_solution(15391384696929211790)
XLA Ops:
  8.7 32.5 %all_gather.12 = bf16[64,8,256]{2,1,0:T(8,128)(2,1)S(1)} all-gather(bf16[8,8,256]{2,1,0:T(8,128)(2,1)S(1)} %convert_element_type.40), channel_id=1, replica_groups=mesh['grp'=2,'aux'=8,'tr'=2] {'aux'}, dimensions={0}, use_global_device_ids=true | all-gather | bytes 294912 | tf_op jit(solution)/shard_map/all_gather | solution.py:13
  41.5 37.3 %while.20 = (s32[]{:T(128)}, f32[64,8,512]{2,1,0:T(8,128)S(1)}, s32[]{:T(128)}, bf16[64,64,64]{2,1,0:T(8,128)(2,1)}, bf16[64,8,256]{2,0,1:T(8,128)(2,1)S(1)}, /*...) while((s32[]{:T(128)}, f32[64,8,512]{2,1,0:T(8,128)S(1)}, ...), condition=%wide.region_1.2_spmd, body=%wide.region_0.1_spmd.sunk | while | flops 1210318848 | bytes 8782059 | solution.py:40
  41.5 1.7 multiply_convert_fusion.4
  43.2 3.0 fusion.69
  46.3 1.6 multiply_convert_fusion.4
  47.9 3.0 fusion.69
  50.9 1.6 multiply_convert_fusion.4
  52.5 3.0 fusion.69
  55.6 1.6 multiply_convert_fusion.4
  57.2 3.0 fusion.69
  60.2 1.6 multiply_convert_fusion.4
  61.8 3.0 fusion.69
  64.9 1.6 multiply_convert_fusion.4
  66.5 3.0 fusion.69
  69.5 1.6 multiply_convert_fusion.4
  71.1 3.0 fusion.69
  74.2 1.6 multiply_convert_fusion.4
  75.8 3.0 fusion.69
  79.8 18.8 %reduce-scatter.5.cloned.1.call-done = f32[64,8,256]{2,1,0:T(8,128)} async-done(((f32[64,8,512]{2,1,0:T(8,128)}), f32[64,8,256]{2,1,0:T(8,128)}) %reduce-scatter.5.cloned.1.call-update) | async-done | bytes 524304 | tf_op jit(solution)/shard_map/reduce_scatter | solution.py:41
  98.7 75.8 %psum.28 = bf16[8,512]{1,0:T(8,128)(2,1)S(1)} all-reduce(f32[8,512]{1,0:T(8,128)S(1)} %get-tuple-element.318), channel_id=1, replica_groups=mesh['grp'=2,'aux'=8,'tr'=2] {'aux','tr'}, use_global_device_ids=true, to_apply=%region_6.7 | all-reduce | flops 4096 | bytes 24576 | tf_op jit(solution)/shard_map/psum | solution.py:49
  174.6 1.5 add.75
  176.2 13.6 %all-reduce.3.cloned.1.call-done = f32[8,8,256]{2,1,0:T(8,128)} async-done(((f32[8,8,256]{2,1,0:T(8,128)}), f32[8,8,256]{2,1,0:T(8,128)}) %all-reduce.3.cloned.1.call-update) | async-done | bytes 65552 | tf_op jit(solution)/shard_map/psum | solution.py:58
  189.8 1.0 convolution_bitcast_fusion.5
  190.9 41.4 %all-gather = f32[128,8]{1,0:T(8,128)S(1)} all-gather(f32[8,8]{1,0:T(8,128)S(1)} %copy.14), channel_id=2, replica_groups=mesh['grp'=2,'aux'=8,'tr'=2] {'aux','tr'}, dimensions={0}, use_global_device_ids=true | all-gather | bytes 4352 | tf_op jit(solution)/shard_map/all_gather | solution.py:70
  232.4 1.0 fusion.46
  233.4 30.8 %all_gather.15 = bf16[64,8,256]{2,1,0:T(8,128)(2,1)S(1)} all-gather(bf16[8,8,256]{2,1,0:T(8,128)(2,1)S(1)} %get-tuple-element.162), channel_id=1, replica_groups=mesh['grp'=2,'aux'=8,'tr'=2] {'aux'}, dimensions={0}, use_global_device_ids=true | all-gather | bytes 294912 | tf_op jit(solution)/shard_map/all_gather | solution.py:13
  264.4 37.2 %while.21 = (s32[]{:T(128)}, f32[64,8,512]{2,1,0:T(8,128)S(1)}, s32[]{:T(128)}, bf16[64,64,64]{2,1,0:T(8,128)(2,1)}, bf16[64,8,256]{2,0,1:T(8,128)(2,1)S(1)}, /*...) while((s32[]{:T(128)}, f32[64,8,512]{2,1,0:T(8,128)S(1)}, ...), condition=%wide.region_12.13_spmd, body=%wide.region_11.12_spmd.sunk | while | flops 1210318848 | bytes 8782059 | solution.py:40
  264.4 1.6 multiply_convert_fusion.5
  266.0 3.0 fusion.74
  269.0 1.6 multiply_convert_fusion.5
  270.6 3.0 fusion.74
  273.7 1.6 multiply_convert_fusion.5
  275.3 3.0 fusion.74
  278.3 1.6 multiply_convert_fusion.5
  279.9 3.0 fusion.74
  283.0 1.6 multiply_convert_fusion.5
  284.6 3.0 fusion.74
  287.6 1.6 multiply_convert_fusion.5
  289.2 3.0 fusion.74
  292.3 1.6 multiply_convert_fusion.5
  293.9 3.0 fusion.74
  296.9 1.6 multiply_convert_fusion.5
  298.5 3.0 fusion.74
  302.6 16.4 %reduce-scatter.9.cloned.1.call-done = f32[64,8,256]{2,1,0:T(8,128)} async-done(((f32[64,8,512]{2,1,0:T(8,128)}), f32[64,8,256]{2,1,0:T(8,128)}) %reduce-scatter.9.cloned.1.call-update) | async-done | bytes 524304 | tf_op jit(solution)/shard_map/reduce_scatter | solution.py:41
  319.0 76.0 %psum.30 = bf16[8,512]{1,0:T(8,128)(2,1)S(1)} all-reduce(f32[8,512]{1,0:T(8,128)S(1)} %get-tuple-element.320), channel_id=1, replica_groups=mesh['grp'=2,'aux'=8,'tr'=2] {'aux','tr'}, use_global_device_ids=true, to_apply=%region_17.18 | all-reduce | flops 4096 | bytes 24576 | tf_op jit(solution)/shard_map/psum | solution.py:49
  395.0 1.5 add.77
  397.2 13.1 %all-reduce.5.cloned.1.call-done = f32[8,8,256]{2,1,0:T(8,128)} async-done(((f32[8,8,256]{2,1,0:T(8,128)}), f32[8,8,256]{2,1,0:T(8,128)}) %all-reduce.5.cloned.1.call-update) | async-done | bytes 65552 | tf_op jit(solution)/shard_map/psum | solution.py:58
  410.3 1.5 multiply_add_fusion
  (61 shorter events, 4.5 us)
Async XLA Ops:
  7.2 91.4 %reduce-scatter.5.cloned.1.call-start = ((), (), s32[]{:S(2)}) async-start(), calls=%async_computation.4 | async-start | bytes 1572864 | tf_op jit(solution)/shard_map/reduce_scatter | solution.py:41
  41.5 57.2 %copy-start = (bf16[8,256,512]{2,1,0:T(8,128)(2,1)S(1)}, bf16[8,256,512]{2,1,0:T(8,128)(2,1)}, u32[]{:S(2)}) copy-start(bf16[8,256,512]{2,1,0:T(8,128)(2,1)} %param.24) | copy-start | bytes 6291460
  78.8 1.0 copy-start.2
  79.8 94.8 %reduce-scatter.7.cloned.1.call-start = ((), (), s32[]{:S(2)}) async-start(), calls=%async_computation.5 | async-start | bytes 589824 | tf_op jit(solution)/shard_map/reduce_scatter | solution.py:42
  98.6 91.2 %all-reduce.3.cloned.1.call-start = ((), (), s32[]{:S(2)}) async-start(), calls=%async_computation.6 | async-start | bytes 131072 | tf_op jit(solution)/shard_map/psum | solution.py:58
  98.7 77.5 %copy-start.4 = (f32[256]{0:T(256)S(1)}, f32[256]{0:T(256)}, u32[]{:S(2)}) copy-start(f32[256]{0:T(256)} %param.21) | copy-start | bytes 3076
  98.7 77.5 %copy-start.5 = (f32[8]{0:T(128)S(1)}, f32[8]{0:T(128)}, u32[]{:S(2)}) copy-start(f32[8]{0:T(128)} %param.20) | copy-start | bytes 100
  98.7 91.1 %copy-start.3 = (f32[8,8,256]{2,1,0:T(8,128)S(1)}, f32[8,8,256]{2,1,0:T(8,128)}, u32[]{:S(2)}) copy-start(f32[8,8,256]{2,1,0:T(8,128)} %param.19) | copy-start | bytes 196612
  176.1 142.9 %reduce-scatter.9.cloned.1.call-start = ((), (), s32[]{:S(2)}) async-start(), calls=%async_computation.7 | async-start | bytes 1572864 | tf_op jit(solution)/shard_map/reduce_scatter | solution.py:41
  301.5 1.0 copy-start.1
  302.5 92.5 %reduce-scatter.11.cloned.1.call-start = ((), (), s32[]{:S(2)}) async-start(), calls=%async_computation.8 | async-start | bytes 589824 | tf_op jit(solution)/shard_map/reduce_scatter | solution.py:42
  319.0 91.3 %all-reduce.5.cloned.1.call-start = ((), (), s32[]{:S(2)}) async-start(), calls=%async_computation.9 | async-start | bytes 131072 | tf_op jit(solution)/shard_map/psum | solution.py:58
Sparse Core Ops, SparseCore 0:
  79.9 18.6 reduce-scatter.4
  101.9 62.7 reduce-scatter.6
  176.2 13.5 all-reduce.2
  302.6 16.2 reduce-scatter.8
  322.1 62.6 reduce-scatter.10
  396.6 13.5 all-reduce.4
